TPU v7x, 256 devices: a whole 4x4x8 slice. The times are simulated.
256 devices in a mesh: cp: 32 (over z_lo, y, core), tp: 8 (over z_hi, x).
Axes of the slice: x: 4, y: 4, z: 8 (z_hi: 2, z_lo: 4; z = z_hi * 4 + z_lo), core: 2. Of those that a mesh axis runs over, the one named last changes fastest.
Arguments:
- tokens: bfloat16 [16384, 4096], P('cp', 'tp'), may hold values from -40 to 40
- span_ids: int32 [32, 2], P('cp'), may hold values from 0 to 63, as said below
- positions: int32 [16384], P('cp'), may hold values from 0 to 8191, as said below
- q_weight: bfloat16 [4096, 4096], P(None, 'tp'), may hold values from -0.09375 to 0.09375
- k_weight: bfloat16 [4096, 1024], P(None, 'tp'), may hold values from -0.09375 to 0.09375
- v_weight: bfloat16 [4096, 1024], P(None, 'tp'), may hold values from -0.09375 to 0.09375
- o_weight: bfloat16 [4096, 4096], P('tp'), may hold values from -0.09375 to 0.09375
Outputs:
- attended: bfloat16 [16384, 4096], P('cp', 'tp')
Inputs may be any that keep to these rules, and one draw needn't show every extreme that they name: `span_ids`: row r names the two spans held by index r of cp: a span c and the span 64 - 1 - c, in either order; every span is named once. Span c covers the places c * (256) to (c + 1) * 256 - 1 of the sequence. `positions`: along the sequence (in the order of places given by span_ids) documents are runs of consecutive tokens; a position is 0 at a document's first token and rises by one up to its last, and the first place of the sequence has position 0.
All inputs are finite; a program needn't handle non-finite values.
Results may differ from a plain program's by a relative error of at most 0.014.
The roundings to bfloat16 on the way count: a program that leaves them out, or rounds other values in their place, can miss the bound.
Values may be sent and summed in bfloat16 or wider, within the bound.
A program may use at most 64 MiB of HBM per device.

v0:
```python
from functools import partial
import jax
import jax.numpy as jnp
from jax import lax
from jax.sharding import Mesh
from jax.sharding import PartitionSpec as P

HD = 128
TP = ("tp_0", "tp_1")
CP = ("cp_0", "cp_1", "cp_2")
theta_base = 500000.0
floor_score = -1e30


def in_order(pieces, dim):
    shape = list(pieces.shape[1:])
    shape[dim] *= pieces.shape[0]
    return jnp.moveaxis(pieces, 0, dim).reshape(shape)


def all_blocks(value, axes, order):
    pieces = value[None]
    for k in order:
        pieces = lax.all_gather(pieces, axes[k], axis=0, tiled=True)
    current = [lax.axis_size(axes[k]) for k in reversed(order)]
    pieces = pieces.reshape(*current, *value.shape)
    turned = sorted(range(len(order)), key=lambda place: order[len(order) - 1 - place])
    return pieces.transpose(*turned, *range(len(order), pieces.ndim)).reshape(-1, *value.shape)


def gather_axes(value, axes, order, dim):
    return in_order(all_blocks(value, axes, order), dim)


def from_behind(block, axis, distance):
    devices = range(lax.axis_size(axis))
    route = [((i - distance) % len(devices), i) for i in devices]
    return lax.ppermute(block, axis, route)


def sum_in_order(pieces, axes, order):
    inside = pieces.shape[1:]
    pieces = pieces.reshape(*(lax.axis_size(a) for a in axes), *inside)
    pieces = jnp.moveaxis(pieces, order, range(len(axes))).reshape(-1, *inside)
    for k in order:
        pieces = lax.psum_scatter(pieces, axes[k], scatter_dimension=0, tiled=True)
    return pieces[0]


def in_blocks(value, dim, length):
    shape = value.shape
    pieces = value.reshape(*shape[:dim], length, shape[dim] // length, *shape[dim + 1 :])
    return jnp.moveaxis(pieces, dim, 0)


def sum_by_axis(value, axes, order, dim):
    length = lax.axis_size(axes)
    return sum_in_order(in_blocks(value, dim, length), axes, order)


def rotate(vectors, positions):
    half_size = vectors.shape[-1] // 2
    exponent = jnp.arange(half_size, dtype=jnp.float32) * (2.0 / vectors.shape[-1])
    inverse_freq = theta_base ** (-exponent)
    angles = positions.astype(jnp.float32)[:, None] * inverse_freq[None, :]
    cosine = jnp.cos(angles)[:, None, :]
    sine_part = jnp.sin(angles)[:, None, :]
    lower_half = vectors[..., :half_size]
    upper_half = vectors[..., half_size:]
    return jnp.concatenate(
        [
            lower_half * cosine - upper_half * sine_part,
            upper_half * cosine + lower_half * sine_part,
        ],
        axis=-1,
    )


def block_update(
    carried, block_queries, query_index, query_start, block_keys, block_values, key_index
):
    row_max, weight_sum, weighted = carried
    scale_factor = block_queries.shape[-1] ** (-0.5)
    scores = (
        jnp.einsum("hrd,kd->hrk", block_queries, block_keys, preferred_element_type=jnp.float32)
        * scale_factor
    )
    visible = (
        (key_index[None, :] <= query_index[:, None]) & (key_index[None, :] >= query_start[:, None])
    )[None]
    scores = jnp.where(visible, scores, floor_score)
    new_max = jnp.maximum(row_max, jnp.max(scores, axis=-1))
    weights = jnp.where(visible, jnp.exp(scores - new_max[..., None]), 0.0)
    rescale = jnp.exp(row_max - new_max)
    weight_sum = weight_sum * rescale + jnp.sum(weights, axis=-1)
    weighted = weighted * rescale[..., None] + jnp.einsum(
        "hrk,kd->hrd",
        weights.astype(jnp.bfloat16),
        block_values,
        preferred_element_type=jnp.float32,
    )
    return (new_max, weight_sum, weighted)


def keep_state(carried):
    return carried


def attend(halves, query_parts, key_block, value_block, key_index):
    half_rows = key_block.shape[0] // 2
    updated = []
    for query_half in range(2):
        carried = halves[query_half]
        block_queries, query_index, query_start = query_parts[query_half]
        lowest_start = jnp.min(query_start)
        for key_half in range(2):
            key_rows = lax.slice_in_dim(
                key_block, key_half * half_rows, (key_half + 1) * half_rows, axis=0
            )
            value_rows = lax.slice_in_dim(
                value_block, key_half * half_rows, (key_half + 1) * half_rows, axis=0
            )
            index_rows = lax.slice_in_dim(
                key_index, key_half * half_rows, (key_half + 1) * half_rows, axis=0
            )
            needed = (index_rows[0] <= query_index[-1]) & (index_rows[-1] >= lowest_start)
            update_fn = partial(
                block_update,
                block_queries=block_queries,
                query_index=query_index,
                query_start=query_start,
                block_keys=key_rows,
                block_values=value_rows,
                key_index=index_rows,
            )
            carried = lax.cond(needed, update_fn, keep_state, carried)
        updated.append(carried)
    return tuple(updated)


def per_device(tokens, span_ids, positions, q_weight, k_weight, v_weight, o_weight):
    row_count = tokens.shape[0]
    half_rows = row_count // 2
    head_count = q_weight.shape[1] // HD
    weights_in = (q_weight, k_weight, v_weight)
    pieces = lax.all_gather(tokens, TP, axis=1, tiled=True)
    queries, keys_here, values_here = tuple(
        (jnp.dot(pieces, matrix, preferred_element_type=jnp.float32) for matrix in weights_in)
    )
    queries = rotate(queries.reshape(row_count, head_count, HD), positions).astype(jnp.bfloat16)
    queries = jnp.transpose(queries, (1, 0, 2))
    keys_here = (
        rotate(keys_here.reshape(row_count, 1, HD), positions)
        .reshape(row_count, HD)
        .astype(jnp.bfloat16)
    )
    values_here = values_here.astype(jnp.bfloat16)
    span_table = gather_axes(span_ids, (("cp_0", "cp_1"), "cp_2"), (0, 1), 0)
    rank_count = span_table.shape[0]
    offsets = jnp.arange(half_rows, dtype=jnp.int32)
    global_index = (span_table[:, :, None] * half_rows + offsets[None, None, :]).reshape(
        rank_count * row_count
    )
    my_rank = lax.axis_index(CP)
    own_index = lax.dynamic_slice_in_dim(global_index, my_rank * row_count, row_count)
    doc_start = own_index - positions
    query_parts = tuple(
        (
            (
                queries[:, part_index * half_rows : (part_index + 1) * half_rows],
                own_index[part_index * half_rows : (part_index + 1) * half_rows],
                doc_start[part_index * half_rows : (part_index + 1) * half_rows],
            )
            for part_index in range(2)
        )
    )
    empty_state = (
        jnp.full((head_count, half_rows), floor_score, jnp.float32),
        jnp.zeros((head_count, half_rows), jnp.float32),
        jnp.zeros((head_count, half_rows, HD), jnp.float32),
    )
    halves = (empty_state, empty_state)
    halves = attend(halves, query_parts, keys_here, values_here, own_index)

    def turn(turn_index, loop_state):
        carried, moving = loop_state
        moving = from_behind(moving, CP, 1)
        source = (my_rank - turn_index - 1) % rank_count
        key_index = lax.dynamic_slice_in_dim(global_index, source * row_count, row_count)
        return (attend(carried, query_parts, moving[0], moving[1], key_index), moving)

    halves, moved_last = lax.fori_loop(
        0, rank_count - 1, turn, (halves, jnp.stack((keys_here, values_here)))
    )
    outputs = []
    for carried in halves:
        outputs.append(carried[2] / carried[1][..., None])
    attention = jnp.concatenate(outputs, axis=1).astype(jnp.bfloat16)
    out_weight = o_weight.reshape(head_count, HD, o_weight.shape[1])
    partial_sum = jnp.einsum(
        "hrd,hdn->rn", attention, out_weight, preferred_element_type=jnp.float32
    )
    return (
        sum_by_axis(partial_sum.astype(jnp.bfloat16), TP, (1, 0), 1)
        .astype(jnp.float32)
        .astype(jnp.bfloat16)
    )


def solution(mesh):
    split = Mesh(mesh.devices.reshape(4, 4, 2, 2, 4), ("cp_0", "cp_1", "cp_2", "tp_0", "tp_1"))
    placed = (P(CP, TP), P(CP, None), P(CP), P(None, TP), P(None, TP), P(None, TP), P(TP, None))
    return jax.shard_map(
        per_device, mesh=split, in_specs=placed, out_specs=P(CP, TP), check_vma=False
    )
```

profile of v0, /device:TPU:1, one launch (start us, length us, event | category | flops | bytes accessed | tf_op | source)
XLA Modules:
  0.0 774.9 jit_solution(6277096617553391568)
XLA Ops:
  7.3 39.4 %all-gather.2 = s32[16,1,2]{2,1,0:T(1,128)S(1)} all-gather(s32[1,1,2]{2,1,0:T(1,128)} %bitcast.155), channel_id=2, replica_groups=mesh['cp_0'=4,'cp_1'=4,'cp_2'=2,'tp_0'=2,'tp_1'=4] {'cp_0','cp_1'}, dimensions={0}, use_global_device_ids=true | all-gather | bytes 136 | tf_op jit(solution)/shard_map/all_gather | solution.py:24
  46.8 7.9 %all-gather.3 = s32[2,16,2]{1,2,0:T(2,128)S(1)} all-gather(s32[1,16,2]{1,2,0:T(2,128)S(1)} %bitcast.154), channel_id=3, replica_groups=mesh['cp_0'=4,'cp_1'=4,'cp_2'=2,'tp_0'=2,'tp_1'=4] {'cp_2'}, dimensions={0}, use_global_device_ids=true | all-gather | bytes 384 | tf_op jit(solution)/shard_map/all_gather | solution.py:24
  69.2 53.8 %all-gather.6.cloned.1.call-done = bf16[512,4096]{1,0:T(8,128)(2,1)} async-done(((bf16[512,512]{1,0:T(8,128)(2,1)}), bf16[512,4096]{1,0:T(8,128)(2,1)}) %all-gather.6.cloned.1.call-update) | async-done | bytes 4194320 | tf_op jit(solution)/shard_map/all_gather | solution.py:146
  123.0 3.8 convolution_bitcast_fusion
  137.5 3.8 conditional.8
  142.0 3.2 conditional.11
  145.2 510.1 %while.27 = (s32[]{:T(128)}, f32[4,256]{1,0:T(4,128)}, f32[4,256]{1,0:T(4,128)S(1)}, f32[4,256,128]{2,1,0:T(8,128)S(1)}, f32[4,256]{1,0:T(4,128)}, /*index=5*/f3...) while((s32[]{:T(128)}, f32[4,256]{1,0:T(4,128)}, ...), condition=%wide.region_35.36_spmd, body=%wide.region_18.35_spmd.sunk | while | flops 548151296 | bytes 21779492 | solution.py:192
  145.2 3.2 collective-permute-start
  192.4 3.2 conditional.19
  275.9 3.2 conditional.19
  357.3 3.2 conditional.19
  405.3 3.2 conditional.19
  424.0 3.2 conditional.18
  456.0 3.2 conditional.19
  504.0 3.2 conditional.18
  535.9 3.2 conditional.17
  583.8 3.2 conditional.19
  635.5 3.8 collective-permute-start
  655.7 5.1 bitcast_convert_fusion
  660.8 4.2 copy.110
  665.0 6.9 reshape.630
  671.9 5.5 copy.79
  677.5 47.7 %reduce-scatter.3.cloned.1.call-done = bf16[2,512,512]{2,1,0:T(8,128)(2,1)} async-done(((bf16[8,512,512]{2,1,0:T(8,128)(2,1)}), bf16[2,512,512]{2,1,0:T(8,128)(2,1)}) %reduce-scatter.3.cloned.1.call-update) | async-done | bytes 1048592 | tf_op jit(solution)/shard_map/reduce_scatter | solution.py:46
  725.2 43.2 %reduce-scatter.5.cloned.1.call-done = bf16[1,512,512]{2,1,0:T(8,128)(2,1)} async-done(((bf16[2,512,512]{2,1,0:T(8,128)(2,1)}), bf16[1,512,512]{2,1,0:T(8,128)(2,1)}) %reduce-scatter.5.cloned.1.call-update) | async-done | bytes 524304 | tf_op jit(solution)/shard_map/reduce_scatter | solution.py:46
  (661 shorter events, 281.4 us)
Async XLA Ops:
  6.5 116.4 %all-gather.6.cloned.1.call-start = ((), (), s32[]{:S(2)}) async-start(), calls=%async_computation.2 | async-start | bytes 4718592 | tf_op jit(solution)/shard_map/all_gather | solution.py:146
  7.3 717.9 %reduce-scatter.3.cloned.1.call-start = ((), (), s32[]{:S(2)}) async-start(), calls=%async_computation.3 | async-start | bytes 5242880 | tf_op jit(solution)/shard_map/reduce_scatter | solution.py:46
  145.2 15.2 %collective-permute-start = (bf16[2,512,128]{2,1,0:T(8,128)(2,1)}, bf16[2,512,128]{2,1,0:T(8,128)(2,1)S(1)}, u32[]{:S(2)}, u32[]{:S(2)}) collective-permute-start(bf16[2,512,128]{2,1,0:T(8,128)(2,1)} %get-tuple-element.1174), channel_id=1, source_target_pairs={{248,0},{0,8},{8,16},{16,24},{24,32},{32,40},{40,48},{48,56},{56,6... | collective-permute-start | bytes 786440 | tf_op jit(solution)/shard_map/while/body/eval_jaxpr/ppermute | solution.py:38
  164.3 12.0 %collective-permute-start = (bf16[2,512,128]{2,1,0:T(8,128)(2,1)}, bf16[2,512,128]{2,1,0:T(8,128)(2,1)S(1)}, u32[]{:S(2)}, u32[]{:S(2)}) collective-permute-start(bf16[2,512,128]{2,1,0:T(8,128)(2,1)} %get-tuple-element.1174), channel_id=1, source_target_pairs={{248,0},{0,8},{8,16},{16,24},{24,32},{32,40},{40,48},{48,56},{56,6... | collective-permute-start | bytes 786440 | tf_op jit(solution)/shard_map/while/body/eval_jaxpr/ppermute | solution.py:38
  180.3 12.0 %collective-permute-start = (bf16[2,512,128]{2,1,0:T(8,128)(2,1)}, bf16[2,512,128]{2,1,0:T(8,128)(2,1)S(1)}, u32[]{:S(2)}, u32[]{:S(2)}) collective-permute-start(bf16[2,512,128]{2,1,0:T(8,128)(2,1)} %get-tuple-element.1174), channel_id=1, source_target_pairs={{248,0},{0,8},{8,16},{16,24},{24,32},{32,40},{40,48},{48,56},{56,6... | collective-permute-start | bytes 786440 | tf_op jit(solution)/shard_map/while/body/eval_jaxpr/ppermute | solution.py:38
  196.3 13.5 %collective-permute-start = (bf16[2,512,128]{2,1,0:T(8,128)(2,1)}, bf16[2,512,128]{2,1,0:T(8,128)(2,1)S(1)}, u32[]{:S(2)}, u32[]{:S(2)}) collective-permute-start(bf16[2,512,128]{2,1,0:T(8,128)(2,1)} %get-tuple-element.1174), channel_id=1, source_target_pairs={{248,0},{0,8},{8,16},{16,24},{24,32},{32,40},{40,48},{48,56},{56,6... | collective-permute-start | bytes 786440 | tf_op jit(solution)/shard_map/while/body/eval_jaxpr/ppermute | solution.py:38
  213.8 12.0 %collective-permute-start = (bf16[2,512,128]{2,1,0:T(8,128)(2,1)}, bf16[2,512,128]{2,1,0:T(8,128)(2,1)S(1)}, u32[]{:S(2)}, u32[]{:S(2)}) collective-permute-start(bf16[2,512,128]{2,1,0:T(8,128)(2,1)} %get-tuple-element.1174), channel_id=1, source_target_pairs={{248,0},{0,8},{8,16},{16,24},{24,32},{32,40},{40,48},{48,56},{56,6... | collective-permute-start | bytes 786440 | tf_op jit(solution)/shard_map/while/body/eval_jaxpr/ppermute | solution.py:38
  229.7 13.4 %collective-permute-start = (bf16[2,512,128]{2,1,0:T(8,128)(2,1)}, bf16[2,512,128]{2,1,0:T(8,128)(2,1)S(1)}, u32[]{:S(2)}, u32[]{:S(2)}) collective-permute-start(bf16[2,512,128]{2,1,0:T(8,128)(2,1)} %get-tuple-element.1174), channel_id=1, source_target_pairs={{248,0},{0,8},{8,16},{16,24},{24,32},{32,40},{40,48},{48,56},{56,6... | collective-permute-start | bytes 786440 | tf_op jit(solution)/shard_map/while/body/eval_jaxpr/ppermute | solution.py:38
  247.1 12.0 %collective-permute-start = (bf16[2,512,128]{2,1,0:T(8,128)(2,1)}, bf16[2,512,128]{2,1,0:T(8,128)(2,1)S(1)}, u32[]{:S(2)}, u32[]{:S(2)}) collective-permute-start(bf16[2,512,128]{2,1,0:T(8,128)(2,1)} %get-tuple-element.1174), channel_id=1, source_target_pairs={{248,0},{0,8},{8,16},{16,24},{24,32},{32,40},{40,48},{48,56},{56,6... | collective-permute-start | bytes 786440 | tf_op jit(solution)/shard_map/while/body/eval_jaxpr/ppermute | solution.py:38
  263.1 12.7 %collective-permute-start = (bf16[2,512,128]{2,1,0:T(8,128)(2,1)}, bf16[2,512,128]{2,1,0:T(8,128)(2,1)S(1)}, u32[]{:S(2)}, u32[]{:S(2)}) collective-permute-start(bf16[2,512,128]{2,1,0:T(8,128)(2,1)} %get-tuple-element.1174), channel_id=1, source_target_pairs={{248,0},{0,8},{8,16},{16,24},{24,32},{32,40},{40,48},{48,56},{56,6... | collective-permute-start | bytes 786440 | tf_op jit(solution)/shard_map/while/body/eval_jaxpr/ppermute | solution.py:38
  279.8 12.0 %collective-permute-start = (bf16[2,512,128]{2,1,0:T(8,128)(2,1)}, bf16[2,512,128]{2,1,0:T(8,128)(2,1)S(1)}, u32[]{:S(2)}, u32[]{:S(2)}) collective-permute-start(bf16[2,512,128]{2,1,0:T(8,128)(2,1)} %get-tuple-element.1174), channel_id=1, source_target_pairs={{248,0},{0,8},{8,16},{16,24},{24,32},{32,40},{40,48},{48,56},{56,6... | collective-permute-start | bytes 786440 | tf_op jit(solution)/shard_map/while/body/eval_jaxpr/ppermute | solution.py:38
  295.8 12.0 %collective-permute-start = (bf16[2,512,128]{2,1,0:T(8,128)(2,1)}, bf16[2,512,128]{2,1,0:T(8,128)(2,1)S(1)}, u32[]{:S(2)}, u32[]{:S(2)}) collective-permute-start(bf16[2,512,128]{2,1,0:T(8,128)(2,1)} %get-tuple-element.1174), channel_id=1, source_target_pairs={{248,0},{0,8},{8,16},{16,24},{24,32},{32,40},{40,48},{48,56},{56,6... | collective-permute-start | bytes 786440 | tf_op jit(solution)/shard_map/while/body/eval_jaxpr/ppermute | solution.py:38
  311.8 13.4 %collective-permute-start = (bf16[2,512,128]{2,1,0:T(8,128)(2,1)}, bf16[2,512,128]{2,1,0:T(8,128)(2,1)S(1)}, u32[]{:S(2)}, u32[]{:S(2)}) collective-permute-start(bf16[2,512,128]{2,1,0:T(8,128)(2,1)} %get-tuple-element.1174), channel_id=1, source_target_pairs={{248,0},{0,8},{8,16},{16,24},{24,32},{32,40},{40,48},{48,56},{56,6... | collective-permute-start | bytes 786440 | tf_op jit(solution)/shard_map/while/body/eval_jaxpr/ppermute | solution.py:38
  329.1 12.1 %collective-permute-start = (bf16[2,512,128]{2,1,0:T(8,128)(2,1)}, bf16[2,512,128]{2,1,0:T(8,128)(2,1)S(1)}, u32[]{:S(2)}, u32[]{:S(2)}) collective-permute-start(bf16[2,512,128]{2,1,0:T(8,128)(2,1)} %get-tuple-element.1174), channel_id=1, source_target_pairs={{248,0},{0,8},{8,16},{16,24},{24,32},{32,40},{40,48},{48,56},{56,6... | collective-permute-start | bytes 786440 | tf_op jit(solution)/shard_map/while/body/eval_jaxpr/ppermute | solution.py:38
  345.2 12.0 %collective-permute-start = (bf16[2,512,128]{2,1,0:T(8,128)(2,1)}, bf16[2,512,128]{2,1,0:T(8,128)(2,1)S(1)}, u32[]{:S(2)}, u32[]{:S(2)}) collective-permute-start(bf16[2,512,128]{2,1,0:T(8,128)(2,1)} %get-tuple-element.1174), channel_id=1, source_target_pairs={{248,0},{0,8},{8,16},{16,24},{24,32},{32,40},{40,48},{48,56},{56,6... | collective-permute-start | bytes 786440 | tf_op jit(solution)/shard_map/while/body/eval_jaxpr/ppermute | solution.py:38
  361.2 12.0 %collective-permute-start = (bf16[2,512,128]{2,1,0:T(8,128)(2,1)}, bf16[2,512,128]{2,1,0:T(8,128)(2,1)S(1)}, u32[]{:S(2)}, u32[]{:S(2)}) collective-permute-start(bf16[2,512,128]{2,1,0:T(8,128)(2,1)} %get-tuple-element.1174), channel_id=1, source_target_pairs={{248,0},{0,8},{8,16},{16,24},{24,32},{32,40},{40,48},{48,56},{56,6... | collective-permute-start | bytes 786440 | tf_op jit(solution)/shard_map/while/body/eval_jaxpr/ppermute | solution.py:38
  409.1 14.8 %collective-permute-start = (bf16[2,512,128]{2,1,0:T(8,128)(2,1)}, bf16[2,512,128]{2,1,0:T(8,128)(2,1)S(1)}, u32[]{:S(2)}, u32[]{:S(2)}) collective-permute-start(bf16[2,512,128]{2,1,0:T(8,128)(2,1)} %get-tuple-element.1174), channel_id=1, source_target_pairs={{248,0},{0,8},{8,16},{16,24},{24,32},{32,40},{40,48},{48,56},{56,6... | collective-permute-start | bytes 786440 | tf_op jit(solution)/shard_map/while/body/eval_jaxpr/ppermute | solution.py:38
  443.9 12.1 %collective-permute-start = (bf16[2,512,128]{2,1,0:T(8,128)(2,1)}, bf16[2,512,128]{2,1,0:T(8,128)(2,1)S(1)}, u32[]{:S(2)}, u32[]{:S(2)}) collective-permute-start(bf16[2,512,128]{2,1,0:T(8,128)(2,1)} %get-tuple-element.1174), channel_id=1, source_target_pairs={{248,0},{0,8},{8,16},{16,24},{24,32},{32,40},{40,48},{48,56},{56,6... | collective-permute-start | bytes 786440 | tf_op jit(solution)/shard_map/while/body/eval_jaxpr/ppermute | solution.py:38
  459.9 12.0 %collective-permute-start = (bf16[2,512,128]{2,1,0:T(8,128)(2,1)}, bf16[2,512,128]{2,1,0:T(8,128)(2,1)S(1)}, u32[]{:S(2)}, u32[]{:S(2)}) collective-permute-start(bf16[2,512,128]{2,1,0:T(8,128)(2,1)} %get-tuple-element.1174), channel_id=1, source_target_pairs={{248,0},{0,8},{8,16},{16,24},{24,32},{32,40},{40,48},{48,56},{56,6... | collective-permute-start | bytes 786440 | tf_op jit(solution)/shard_map/while/body/eval_jaxpr/ppermute | solution.py:38
  475.9 12.0 %collective-permute-start = (bf16[2,512,128]{2,1,0:T(8,128)(2,1)}, bf16[2,512,128]{2,1,0:T(8,128)(2,1)S(1)}, u32[]{:S(2)}, u32[]{:S(2)}) collective-permute-start(bf16[2,512,128]{2,1,0:T(8,128)(2,1)} %get-tuple-element.1174), channel_id=1, source_target_pairs={{248,0},{0,8},{8,16},{16,24},{24,32},{32,40},{40,48},{48,56},{56,6... | collective-permute-start | bytes 786440 | tf_op jit(solution)/shard_map/while/body/eval_jaxpr/ppermute | solution.py:38
  539.8 12.0 %collective-permute-start = (bf16[2,512,128]{2,1,0:T(8,128)(2,1)}, bf16[2,512,128]{2,1,0:T(8,128)(2,1)S(1)}, u32[]{:S(2)}, u32[]{:S(2)}) collective-permute-start(bf16[2,512,128]{2,1,0:T(8,128)(2,1)} %get-tuple-element.1174), channel_id=1, source_target_pairs={{248,0},{0,8},{8,16},{16,24},{24,32},{32,40},{40,48},{48,56},{56,6... | collective-permute-start | bytes 786440 | tf_op jit(solution)/shard_map/while/body/eval_jaxpr/ppermute | solution.py:38
  600.5 15.1 %collective-permute-start = (bf16[2,512,128]{2,1,0:T(8,128)(2,1)}, bf16[2,512,128]{2,1,0:T(8,128)(2,1)S(1)}, u32[]{:S(2)}, u32[]{:S(2)}) collective-permute-start(bf16[2,512,128]{2,1,0:T(8,128)(2,1)} %get-tuple-element.1174), channel_id=1, source_target_pairs={{248,0},{0,8},{8,16},{16,24},{24,32},{32,40},{40,48},{48,56},{56,6... | collective-permute-start | bytes 786440 | tf_op jit(solution)/shard_map/while/body/eval_jaxpr/ppermute | solution.py:38
  635.5 15.8 %collective-permute-start = (bf16[2,512,128]{2,1,0:T(8,128)(2,1)}, bf16[2,512,128]{2,1,0:T(8,128)(2,1)S(1)}, u32[]{:S(2)}, u32[]{:S(2)}) collective-permute-start(bf16[2,512,128]{2,1,0:T(8,128)(2,1)} %get-tuple-element.1174), channel_id=1, source_target_pairs={{248,0},{0,8},{8,16},{16,24},{24,32},{32,40},{40,48},{48,56},{56,6... | collective-permute-start | bytes 786440 | tf_op jit(solution)/shard_map/while/body/eval_jaxpr/ppermute | solution.py:38
  677.4 91.0 %reduce-scatter.5.cloned.1.call-start = ((), (), s32[]{:S(2)}) async-start(), calls=%async_computation.4 | async-start | bytes 1572864 | tf_op jit(solution)/shard_map/reduce_scatter | solution.py:46
  (14 other events, 302.8 us)
Sparse Core Ops, SparseCore 0:
  9.8 113.1 all-gather.5
  677.5 47.6 reduce-scatter.2
  727.7 40.6 reduce-scatter.4
where the time goes:
time: 782 us; the launch traced here: 775 us
  loops' own time  314 us (40%)
  waiting for transfers between devices  146 us (19%)
  local copies, waits for them, and re-layouts  124 us (16%)
  other arithmetic  62.2 us (8%)
  blocking collectives  47.4 us (6%)
  matrix products  40.1 us (5%)
  between operations  23.4 us (3%)
  starting transfers between devices  18.2 us (2%)
    another operation x1, loops' own time, per_device(): lax.fori_loop(0, rank_count - 1, turn, (halves, jnp.stack((keys_here, val...  311 us
    reduce_scatter x2, waiting for transfers between devices, sum_in_order(): pieces = lax.psum_scatter(pieces, axes[k], scatter_dimension=0, tiled=True)  90.9 us
    all_gather x1, waiting for transfers between devices, per_device(): pieces = lax.all_gather(tokens, TP, axis=1, tiled=True)  53.8 us
    all_gather x2, blocking collectives, all_blocks(): pieces = lax.all_gather(pieces, axes[k], axis=0, tiled=True)  47.4 us
    slice x62, local copies, waits for them, and re-layouts, attend(): query_index[-1]  38.8 us
    add x32, other arithmetic, block_update(): weight_sum = weight_sum * rescale + jnp.sum(weights, axis=-1)  22.2 us
    while x31, local copies, waits for them, and re-layouts  21.6 us
    max x31, other arithmetic, block_update(): new_max = jnp.maximum(row_max, jnp.max(scores, axis=-1))  21.2 us
  transfers between devices with their start and end apart: 34, of which 3 were waited for; matrix products, arithmetic and copies ran while one was open for 9% of the time, Pallas kernels for 0%

commit v1 on v0

--- a/solution.py
+++ b/solution.py
@@ -143,7 +143,9 @@
     half_rows = row_count // 2
     head_count = q_weight.shape[1] // HD
     weights_in = (q_weight, k_weight, v_weight)
-    pieces = lax.all_gather(tokens, TP, axis=1, tiled=True)
+    pieces = jnp.concatenate(
+        lax.all_to_all(jnp.stack([tokens] * lax.axis_size(TP)), TP, 0, 0), axis=1
+    )
     queries, keys_here, values_here = tuple(
         (jnp.dot(pieces, matrix, preferred_element_type=jnp.float32) for matrix in weights_in)
     )

time: 782 us -> 827 us (1.058)
  blocking collectives: 47.4 us -> 121 us
  waiting for transfers between devices: 146 us -> 99.8 us
  starting transfers between devices: 18.2 us -> 29.8 us
    all_gather x2, blocking collectives: 47.4 us -> 121 us  [all_blocks(): pieces = lax.all_gather(pieces, axes[k], axis=0, tiled=True)]
    all_gather x1 -> x0, waiting for transfers between devices: 53.8 us -> none  [per_device(): pieces = lax.all_gather(tokens, TP, axis=1, tiled=True)]
    while x31, local copies, waits for them, and re-layouts: 21.6 us -> 0.56 us
    reshape x0 -> x3, local copies, waits for them, and re-layouts: none -> 16.7 us  [per_device(): jnp.concatenate(lax.all_to_all(jnp.stack([tokens] * lax.axis_size(TP)), T...]
    all_to_all x0 -> x1, starting transfers between devices: none -> 11.6 us  [per_device(): lax.all_to_all(jnp.stack([tokens] * lax.axis_size(TP)), TP, 0, 0)]
    reduce_scatter x2, waiting for transfers between devices: 90.9 us -> 99.7 us  [sum_in_order(): pieces = lax.psum_scatter(pieces, axes[k], scatter_dimension=0, tiled=True)]
  transfers between devices with their start and end apart: 34 -> 34, of which waited for: 3 -> 2; matrix products, arithmetic and copies ran while one was open for 9% -> 9% of each run, Pallas kernels for 0% -> 0%
where the time goes in v1:
time: 827 us; the launch traced here: 820 us
  loops' own time  317 us (38%)
  local copies, waits for them, and re-layouts  128 us (15%)
  blocking collectives  121 us (15%)
  waiting for transfers between devices  99.8 us (12%)
  other arithmetic  57.9 us (7%)
  matrix products  43.4 us (5%)
  starting transfers between devices  29.8 us (4%)
  between operations  23.3 us (3%)
    another operation x1, loops' own time, per_device(): lax.fori_loop(0, rank_count - 1, turn, (halves, jnp.stack((keys_here, val...  314 us
    all_gather x2, blocking collectives, all_blocks(): pieces = lax.all_gather(pieces, axes[k], axis=0, tiled=True)  121 us
    reduce_scatter x2, waiting for transfers between devices, sum_in_order(): pieces = lax.psum_scatter(pieces, axes[k], scatter_dimension=0, tiled=True)  99.7 us
    slice x62, local copies, waits for them, and re-layouts, attend(): query_index[-1]  39.7 us
    add x32, other arithmetic, block_update(): weight_sum = weight_sum * rescale + jnp.sum(weights, axis=-1)  22.2 us
    max x31, other arithmetic, block_update(): new_max = jnp.maximum(row_max, jnp.max(scores, axis=-1))  21.3 us
    slice x31, local copies, waits for them, and re-layouts, attend(): index_rows[-1] >= lowest_start  20.8 us
    cond x31, local copies, waits for them, and re-layouts  18.4 us
  transfers between devices with their start and end apart: 34, of which 2 were waited for; matrix products, arithmetic and copies ran while one was open for 9% of the time, Pallas kernels for 0%

profile of v1, /device:TPU:1, one launch (start us, length us, event | category | flops | bytes accessed | tf_op | source)
XLA Modules:
  0.0 819.6 jit_solution(2408055725715267972)
XLA Ops:
  6.5 3.5 stack.6
  10.0 11.6 %all-to-all-start = ((bf16[8,512,512]{2,1,0:T(8,128)(2,1)}), bf16[8,512,512]{2,1,0:T(8,128)(2,1)}, u32[]{:S(2)}, u32[]{:S(2)}) async-start(bf16[8,512,512]{2,1,0:T(8,128)(2,1)} %stack.6), calls=%async_computation | async-start | bytes 8388608 | tf_op jit(solution)/shard_map/all_to_all | solution.py:147
  21.7 112.3 %all-gather.2 = s32[16,1,2]{2,1,0:T(1,128)S(1)} all-gather(s32[1,1,2]{2,1,0:T(1,128)S(1)} %bitcast.162), channel_id=2, replica_groups=mesh['cp_0'=4,'cp_1'=4,'cp_2'=2,'tp_0'=2,'tp_1'=4] {'cp_0','cp_1'}, dimensions={0}, use_global_device_ids=true | all-gather | bytes 136 | tf_op jit(solution)/shard_map/all_gather | solution.py:24
  134.0 8.5 %all-gather.3 = s32[2,16,2]{1,2,0:T(2,128)S(1)} all-gather(s32[1,16,2]{1,2,0:T(2,128)S(1)} %bitcast.161), channel_id=3, replica_groups=mesh['cp_0'=4,'cp_1'=4,'cp_2'=2,'tp_0'=2,'tp_1'=4] {'cp_2'}, dimensions={0}, use_global_device_ids=true | all-gather | bytes 384 | tf_op jit(solution)/shard_map/all_gather | solution.py:24
  153.8 6.4 copy.126
  165.7 6.5 copy.77
  172.2 7.5 reshape.669
  179.6 3.7 convolution_convert_fusion
  183.6 5.8 fusion.108
  190.0 3.8 conditional.8
  194.5 3.2 conditional.11
  197.7 493.0 %while.27 = (s32[]{:T(128)}, f32[4,256]{1,0:T(4,128)}, f32[4,256]{1,0:T(4,128)S(1)}, f32[4,256,128]{2,1,0:T(8,128)S(1)}, f32[4,256]{1,0:T(4,128)}, /*index=5*/f3...) while((s32[]{:T(128)}, f32[4,256]{1,0:T(4,128)}, ...), condition=%wide.region_35.36_spmd, body=%wide.region_18.35_spmd.sunk | while | flops 548151296 | bytes 21779492 | solution.py:194
  571.2 3.2 conditional.17
  586.8 3.2 conditional.18
  633.4 6.2 collective-permute-start
  651.8 3.2 conditional.18
  670.5 4.8 collective-permute-start
  687.5 3.2 conditional.19
  691.1 5.1 bitcast_convert_fusion
  696.2 4.2 copy.130
  700.4 6.9 reshape.638
  707.3 5.6 copy.95
  713.0 56.6 %reduce-scatter.3.cloned.1.call-done = bf16[2,512,512]{2,1,0:T(8,128)(2,1)} async-done(((bf16[8,512,512]{2,1,0:T(8,128)(2,1)}), bf16[2,512,512]{2,1,0:T(8,128)(2,1)}) %reduce-scatter.3.cloned.1.call-update) | async-done | bytes 1048592 | tf_op jit(solution)/shard_map/reduce_scatter | solution.py:46
  769.6 43.2 %reduce-scatter.5.cloned.1.call-done = bf16[1,512,512]{2,1,0:T(8,128)(2,1)} async-done(((bf16[2,512,512]{2,1,0:T(8,128)(2,1)}), bf16[1,512,512]{2,1,0:T(8,128)(2,1)}) %reduce-scatter.5.cloned.1.call-update) | async-done | bytes 524304 | tf_op jit(solution)/shard_map/reduce_scatter | solution.py:46
  (668 shorter events, 265.9 us)
Async XLA Ops:
  10.0 150.7 %all-to-all-start = ((bf16[8,512,512]{2,1,0:T(8,128)(2,1)}), bf16[8,512,512]{2,1,0:T(8,128)(2,1)}, u32[]{:S(2)}, u32[]{:S(2)}) async-start(bf16[8,512,512]{2,1,0:T(8,128)(2,1)} %stack.6), calls=%async_computation | async-start | bytes 8388608 | tf_op jit(solution)/shard_map/all_to_all | solution.py:147
  21.6 748.0 %reduce-scatter.3.cloned.1.call-start = ((), (), s32[]{:S(2)}) async-start(), calls=%async_computation.3 | async-start | bytes 5242880 | tf_op jit(solution)/shard_map/reduce_scatter | solution.py:46
  197.7 12.8 %collective-permute-start = (bf16[2,512,128]{2,1,0:T(8,128)(2,1)S(1)}, bf16[2,512,128]{2,1,0:T(8,128)(2,1)S(1)}, u32[]{:S(2)}, u32[]{:S(2)}) collective-permute-start(bf16[2,512,128]{2,1,0:T(8,128)(2,1)S(1)} %get-tuple-element.1172), channel_id=1, source_target_pairs={{248,0},{0,8},{8,16},{16,24},{24,32},{32,40},{40,48},{48,56},{56,6... | collective-permute-start | bytes 786440 | tf_op jit(solution)/shard_map/while/body/eval_jaxpr/ppermute | solution.py:38
  213.8 12.2 %collective-permute-start = (bf16[2,512,128]{2,1,0:T(8,128)(2,1)S(1)}, bf16[2,512,128]{2,1,0:T(8,128)(2,1)S(1)}, u32[]{:S(2)}, u32[]{:S(2)}) collective-permute-start(bf16[2,512,128]{2,1,0:T(8,128)(2,1)S(1)} %get-tuple-element.1172), channel_id=1, source_target_pairs={{248,0},{0,8},{8,16},{16,24},{24,32},{32,40},{40,48},{48,56},{56,6... | collective-permute-start | bytes 786440 | tf_op jit(solution)/shard_map/while/body/eval_jaxpr/ppermute | solution.py:38
  229.3 12.2 %collective-permute-start = (bf16[2,512,128]{2,1,0:T(8,128)(2,1)S(1)}, bf16[2,512,128]{2,1,0:T(8,128)(2,1)S(1)}, u32[]{:S(2)}, u32[]{:S(2)}) collective-permute-start(bf16[2,512,128]{2,1,0:T(8,128)(2,1)S(1)} %get-tuple-element.1172), channel_id=1, source_target_pairs={{248,0},{0,8},{8,16},{16,24},{24,32},{32,40},{40,48},{48,56},{56,6... | collective-permute-start | bytes 786440 | tf_op jit(solution)/shard_map/while/body/eval_jaxpr/ppermute | solution.py:38
  244.9 12.2 %collective-permute-start = (bf16[2,512,128]{2,1,0:T(8,128)(2,1)S(1)}, bf16[2,512,128]{2,1,0:T(8,128)(2,1)S(1)}, u32[]{:S(2)}, u32[]{:S(2)}) collective-permute-start(bf16[2,512,128]{2,1,0:T(8,128)(2,1)S(1)} %get-tuple-element.1172), channel_id=1, source_target_pairs={{248,0},{0,8},{8,16},{16,24},{24,32},{32,40},{40,48},{48,56},{56,6... | collective-permute-start | bytes 786440 | tf_op jit(solution)/shard_map/while/body/eval_jaxpr/ppermute | solution.py:38
  260.4 12.2 %collective-permute-start = (bf16[2,512,128]{2,1,0:T(8,128)(2,1)S(1)}, bf16[2,512,128]{2,1,0:T(8,128)(2,1)S(1)}, u32[]{:S(2)}, u32[]{:S(2)}) collective-permute-start(bf16[2,512,128]{2,1,0:T(8,128)(2,1)S(1)} %get-tuple-element.1172), channel_id=1, source_target_pairs={{248,0},{0,8},{8,16},{16,24},{24,32},{32,40},{40,48},{48,56},{56,6... | collective-permute-start | bytes 786440 | tf_op jit(solution)/shard_map/while/body/eval_jaxpr/ppermute | solution.py:38
  275.9 12.2 %collective-permute-start = (bf16[2,512,128]{2,1,0:T(8,128)(2,1)S(1)}, bf16[2,512,128]{2,1,0:T(8,128)(2,1)S(1)}, u32[]{:S(2)}, u32[]{:S(2)}) collective-permute-start(bf16[2,512,128]{2,1,0:T(8,128)(2,1)S(1)} %get-tuple-element.1172), channel_id=1, source_target_pairs={{248,0},{0,8},{8,16},{16,24},{24,32},{32,40},{40,48},{48,56},{56,6... | collective-permute-start | bytes 786440 | tf_op jit(solution)/shard_map/while/body/eval_jaxpr/ppermute | solution.py:38
  291.5 12.2 %collective-permute-start = (bf16[2,512,128]{2,1,0:T(8,128)(2,1)S(1)}, bf16[2,512,128]{2,1,0:T(8,128)(2,1)S(1)}, u32[]{:S(2)}, u32[]{:S(2)}) collective-permute-start(bf16[2,512,128]{2,1,0:T(8,128)(2,1)S(1)} %get-tuple-element.1172), channel_id=1, source_target_pairs={{248,0},{0,8},{8,16},{16,24},{24,32},{32,40},{40,48},{48,56},{56,6... | collective-permute-start | bytes 786440 | tf_op jit(solution)/shard_map/while/body/eval_jaxpr/ppermute | solution.py:38
  307.0 13.2 %collective-permute-start = (bf16[2,512,128]{2,1,0:T(8,128)(2,1)S(1)}, bf16[2,512,128]{2,1,0:T(8,128)(2,1)S(1)}, u32[]{:S(2)}, u32[]{:S(2)}) collective-permute-start(bf16[2,512,128]{2,1,0:T(8,128)(2,1)S(1)} %get-tuple-element.1172), channel_id=1, source_target_pairs={{248,0},{0,8},{8,16},{16,24},{24,32},{32,40},{40,48},{48,56},{56,6... | collective-permute-start | bytes 786440 | tf_op jit(solution)/shard_map/while/body/eval_jaxpr/ppermute | solution.py:38
  323.5 12.2 %collective-permute-start = (bf16[2,512,128]{2,1,0:T(8,128)(2,1)S(1)}, bf16[2,512,128]{2,1,0:T(8,128)(2,1)S(1)}, u32[]{:S(2)}, u32[]{:S(2)}) collective-permute-start(bf16[2,512,128]{2,1,0:T(8,128)(2,1)S(1)} %get-tuple-element.1172), channel_id=1, source_target_pairs={{248,0},{0,8},{8,16},{16,24},{24,32},{32,40},{40,48},{48,56},{56,6... | collective-permute-start | bytes 786440 | tf_op jit(solution)/shard_map/while/body/eval_jaxpr/ppermute | solution.py:38
  339.1 12.2 %collective-permute-start = (bf16[2,512,128]{2,1,0:T(8,128)(2,1)S(1)}, bf16[2,512,128]{2,1,0:T(8,128)(2,1)S(1)}, u32[]{:S(2)}, u32[]{:S(2)}) collective-permute-start(bf16[2,512,128]{2,1,0:T(8,128)(2,1)S(1)} %get-tuple-element.1172), channel_id=1, source_target_pairs={{248,0},{0,8},{8,16},{16,24},{24,32},{32,40},{40,48},{48,56},{56,6... | collective-permute-start | bytes 786440 | tf_op jit(solution)/shard_map/while/body/eval_jaxpr/ppermute | solution.py:38
  354.6 13.6 %collective-permute-start = (bf16[2,512,128]{2,1,0:T(8,128)(2,1)S(1)}, bf16[2,512,128]{2,1,0:T(8,128)(2,1)S(1)}, u32[]{:S(2)}, u32[]{:S(2)}) collective-permute-start(bf16[2,512,128]{2,1,0:T(8,128)(2,1)S(1)} %get-tuple-element.1172), channel_id=1, source_target_pairs={{248,0},{0,8},{8,16},{16,24},{24,32},{32,40},{40,48},{48,56},{56,6... | collective-permute-start | bytes 786440 | tf_op jit(solution)/shard_map/while/body/eval_jaxpr/ppermute | solution.py:38
  371.4 12.3 %collective-permute-start = (bf16[2,512,128]{2,1,0:T(8,128)(2,1)S(1)}, bf16[2,512,128]{2,1,0:T(8,128)(2,1)S(1)}, u32[]{:S(2)}, u32[]{:S(2)}) collective-permute-start(bf16[2,512,128]{2,1,0:T(8,128)(2,1)S(1)} %get-tuple-element.1172), channel_id=1, source_target_pairs={{248,0},{0,8},{8,16},{16,24},{24,32},{32,40},{40,48},{48,56},{56,6... | collective-permute-start | bytes 786440 | tf_op jit(solution)/shard_map/while/body/eval_jaxpr/ppermute | solution.py:38
  387.0 12.2 %collective-permute-start = (bf16[2,512,128]{2,1,0:T(8,128)(2,1)S(1)}, bf16[2,512,128]{2,1,0:T(8,128)(2,1)S(1)}, u32[]{:S(2)}, u32[]{:S(2)}) collective-permute-start(bf16[2,512,128]{2,1,0:T(8,128)(2,1)S(1)} %get-tuple-element.1172), channel_id=1, source_target_pairs={{248,0},{0,8},{8,16},{16,24},{24,32},{32,40},{40,48},{48,56},{56,6... | collective-permute-start | bytes 786440 | tf_op jit(solution)/shard_map/while/body/eval_jaxpr/ppermute | solution.py:38
  402.6 12.2 %collective-permute-start = (bf16[2,512,128]{2,1,0:T(8,128)(2,1)S(1)}, bf16[2,512,128]{2,1,0:T(8,128)(2,1)S(1)}, u32[]{:S(2)}, u32[]{:S(2)}) collective-permute-start(bf16[2,512,128]{2,1,0:T(8,128)(2,1)S(1)} %get-tuple-element.1172), channel_id=1, source_target_pairs={{248,0},{0,8},{8,16},{16,24},{24,32},{32,40},{40,48},{48,56},{56,6... | collective-permute-start | bytes 786440 | tf_op jit(solution)/shard_map/while/body/eval_jaxpr/ppermute | solution.py:38
  449.1 13.3 %collective-permute-start = (bf16[2,512,128]{2,1,0:T(8,128)(2,1)S(1)}, bf16[2,512,128]{2,1,0:T(8,128)(2,1)S(1)}, u32[]{:S(2)}, u32[]{:S(2)}) collective-permute-start(bf16[2,512,128]{2,1,0:T(8,128)(2,1)S(1)} %get-tuple-element.1172), channel_id=1, source_target_pairs={{248,0},{0,8},{8,16},{16,24},{24,32},{32,40},{40,48},{48,56},{56,6... | collective-permute-start | bytes 786440 | tf_op jit(solution)/shard_map/while/body/eval_jaxpr/ppermute | solution.py:38
  481.3 12.3 %collective-permute-start = (bf16[2,512,128]{2,1,0:T(8,128)(2,1)S(1)}, bf16[2,512,128]{2,1,0:T(8,128)(2,1)S(1)}, u32[]{:S(2)}, u32[]{:S(2)}) collective-permute-start(bf16[2,512,128]{2,1,0:T(8,128)(2,1)S(1)} %get-tuple-element.1172), channel_id=1, source_target_pairs={{248,0},{0,8},{8,16},{16,24},{24,32},{32,40},{40,48},{48,56},{56,6... | collective-permute-start | bytes 786440 | tf_op jit(solution)/shard_map/while/body/eval_jaxpr/ppermute | solution.py:38
  496.9 12.2 %collective-permute-start = (bf16[2,512,128]{2,1,0:T(8,128)(2,1)S(1)}, bf16[2,512,128]{2,1,0:T(8,128)(2,1)S(1)}, u32[]{:S(2)}, u32[]{:S(2)}) collective-permute-start(bf16[2,512,128]{2,1,0:T(8,128)(2,1)S(1)} %get-tuple-element.1172), channel_id=1, source_target_pairs={{248,0},{0,8},{8,16},{16,24},{24,32},{32,40},{40,48},{48,56},{56,6... | collective-permute-start | bytes 786440 | tf_op jit(solution)/shard_map/while/body/eval_jaxpr/ppermute | solution.py:38
  512.4 12.2 %collective-permute-start = (bf16[2,512,128]{2,1,0:T(8,128)(2,1)S(1)}, bf16[2,512,128]{2,1,0:T(8,128)(2,1)S(1)}, u32[]{:S(2)}, u32[]{:S(2)}) collective-permute-start(bf16[2,512,128]{2,1,0:T(8,128)(2,1)S(1)} %get-tuple-element.1172), channel_id=1, source_target_pairs={{248,0},{0,8},{8,16},{16,24},{24,32},{32,40},{40,48},{48,56},{56,6... | collective-permute-start | bytes 786440 | tf_op jit(solution)/shard_map/while/body/eval_jaxpr/ppermute | solution.py:38
  574.5 12.2 %collective-permute-start = (bf16[2,512,128]{2,1,0:T(8,128)(2,1)S(1)}, bf16[2,512,128]{2,1,0:T(8,128)(2,1)S(1)}, u32[]{:S(2)}, u32[]{:S(2)}) collective-permute-start(bf16[2,512,128]{2,1,0:T(8,128)(2,1)S(1)} %get-tuple-element.1172), channel_id=1, source_target_pairs={{248,0},{0,8},{8,16},{16,24},{24,32},{32,40},{40,48},{48,56},{56,6... | collective-permute-start | bytes 786440 | tf_op jit(solution)/shard_map/while/body/eval_jaxpr/ppermute | solution.py:38
  633.4 18.3 %collective-permute-start = (bf16[2,512,128]{2,1,0:T(8,128)(2,1)S(1)}, bf16[2,512,128]{2,1,0:T(8,128)(2,1)S(1)}, u32[]{:S(2)}, u32[]{:S(2)}) collective-permute-start(bf16[2,512,128]{2,1,0:T(8,128)(2,1)S(1)} %get-tuple-element.1172), channel_id=1, source_target_pairs={{248,0},{0,8},{8,16},{16,24},{24,32},{32,40},{40,48},{48,56},{56,6... | collective-permute-start | bytes 786440 | tf_op jit(solution)/shard_map/while/body/eval_jaxpr/ppermute | solution.py:38
  670.5 16.9 %collective-permute-start = (bf16[2,512,128]{2,1,0:T(8,128)(2,1)S(1)}, bf16[2,512,128]{2,1,0:T(8,128)(2,1)S(1)}, u32[]{:S(2)}, u32[]{:S(2)}) collective-permute-start(bf16[2,512,128]{2,1,0:T(8,128)(2,1)S(1)} %get-tuple-element.1172), channel_id=1, source_target_pairs={{248,0},{0,8},{8,16},{16,24},{24,32},{32,40},{40,48},{48,56},{56,6... | collective-permute-start | bytes 786440 | tf_op jit(solution)/shard_map/while/body/eval_jaxpr/ppermute | solution.py:38
  713.0 99.8 %reduce-scatter.5.cloned.1.call-start = ((), (), s32[]{:S(2)}) async-start(), calls=%async_computation.4 | async-start | bytes 1572864 | tf_op jit(solution)/shard_map/reduce_scatter | solution.py:46
  (16 other events, 538.5 us)
Sparse Core Ops, SparseCore 0:
  713.1 56.4 reduce-scatter.2
  772.1 40.6 reduce-scatter.4
